TPU v7x, 512 devices: a whole 4x8x8 slice. The times are simulated.
512 devices in a mesh: dp: 32 (over z, y_hi), tensor: 16 (over x, y_lo, core).
Axes of the slice: x: 4, y: 8 (y_hi: 4, y_lo: 2; y = y_hi * 2 + y_lo), z: 8, core: 2. Of those that a mesh axis runs over, the one named last changes fastest.
Arguments:
- hidden: bfloat16 [16384, 7168], P('dp', 'tensor'), may hold values from -6 to 6
- w_down: bfloat16 [7168, 576], P('tensor'), may hold values from -0.0625 to 0.0625
- norm_gain: float32 [512], replicated, may hold values from 0.25 to 1.75
- w_up: bfloat16 [512, 32768], P('dp', 'tensor'), may hold values from -0.25 to 0.25
- kv_grad: bfloat16 [16384, 32768], P('dp', 'tensor'), may hold values from -6 to 6
- rope_grad: bfloat16 [16384, 64], P('dp'), may hold values from -6 to 6
Outputs:
- hidden_grad: bfloat16 [16384, 7168], P('dp', 'tensor')
- down_grad: bfloat16 [7168, 576], P('tensor')
- gain_grad: float32 [512], replicated
- up_grad: bfloat16 [512, 32768], P('dp', 'tensor')
All inputs are finite; a program needn't handle non-finite values.
Results may differ from a plain program's by a relative error of at most 0.005.
Values may be sent and summed in bfloat16 or wider, within the bound.
No kernel may reach another device: no remote copies, remote signals or barrier semaphores. Data moves between devices by JAX's collectives and lax.ppermute only.
A program may use at most 64 MiB of HBM per device.

v0:
```python
import jax
import jax.numpy as jnp
from jax import lax
from jax.sharding import PartitionSpec as P

MB = 256
MICROS = 2


def norm_back(projected, latent_grad, norm_gain, lat_width):
    inv_rms = lax.rsqrt(jnp.mean(projected * projected, axis=1, keepdims=True) + 1e-06)
    latent = (projected * inv_rms * norm_gain).astype(jnp.bfloat16)
    gain_share = jnp.sum(latent_grad * projected * inv_rms, axis=0)
    scaled = norm_gain * latent_grad
    proj_grad = (
        inv_rms * scaled
        - projected
        * inv_rms
        * inv_rms
        * inv_rms
        * jnp.sum(scaled * projected, axis=1, keepdims=True)
        / lat_width
    ).astype(jnp.bfloat16)
    return (latent, proj_grad, gain_share)


def shards(hidden, w_down, norm_gain, w_up, kv_grad, rope_grad):
    lat_width = norm_gain.shape[0]
    latent_grad_all = lax.dot_general(
        kv_grad,
        lax.all_gather(w_up, "dp", axis=0, tiled=True),
        (((1,), (1,)), ((), ())),
        preferred_element_type=jnp.float32,
    )
    up_running = jnp.zeros((lat_width, kv_grad.shape[1]), jnp.float32)
    down_running = jnp.zeros((w_down.shape[0], w_down.shape[1]), jnp.float32)
    gain_running = jnp.zeros((lat_width,), jnp.float32)
    input_grads = []
    for micro_index in range(MICROS):
        row_range = slice(micro_index * MB, (micro_index + 1) * MB)
        hidden_rows = hidden[row_range]
        cot_rows = kv_grad[row_range]
        proj_partial = jnp.dot(
            hidden_rows, w_down[:, :lat_width], preferred_element_type=jnp.float32
        )
        proj_full, lgrad_full = lax.psum((proj_partial, latent_grad_all[row_range]), "tensor")
        latent, proj_grad, gain_share = norm_back(proj_full, lgrad_full, norm_gain, lat_width)
        gain_running = gain_running + gain_share
        up_running = up_running + lax.dot_general(
            latent, cot_rows, (((0,), (0,)), ((), ())), preferred_element_type=jnp.float32
        )
        joint_grad = jnp.concatenate([proj_grad, rope_grad[row_range]], axis=1)
        down_running = down_running + lax.dot_general(
            hidden_rows, joint_grad, (((0,), (0,)), ((), ())), preferred_element_type=jnp.float32
        )
        input_grads.append(
            lax.dot_general(
                joint_grad, w_down, (((1,), (1,)), ((), ())), preferred_element_type=jnp.float32
            ).astype(jnp.bfloat16)
        )
    hidden_grad = jnp.concatenate(input_grads, axis=0)
    gain_grad = lax.psum(gain_running, "dp")
    up_grad = lax.psum_scatter(up_running, "dp", scatter_dimension=0, tiled=True).astype(
        jnp.bfloat16
    )
    down_grad = lax.psum(down_running, "dp").astype(jnp.bfloat16)
    return (hidden_grad, down_grad, gain_grad, up_grad)


def solution(mesh):
    placed = (
        P("dp", "tensor"),
        P("tensor", None),
        P(),
        P("dp", "tensor"),
        P("dp", "tensor"),
        P("dp", None),
    )
    return jax.shard_map(
        shards,
        mesh=mesh,
        in_specs=placed,
        out_specs=(P("dp", "tensor"), P("tensor", None), P(), P("dp", "tensor")),
        check_vma=False,
    )
```

profile of v0, /device:TPU:2, one launch (start us, length us, event | category | flops | bytes accessed | tf_op | source)
XLA Modules:
  0.0 486.4 jit_solution(1724037319380611540)
XLA Ops:
  7.2 0.7 all-gather.2.cloned.1.call-update
  8.0 2.3 fusion.4
  10.2 2.3 fusion.6
  12.5 89.5 %all-gather.2.cloned.1.call-done = bf16[512,2048]{1,0:T(8,128)(2,1)} async-done(((bf16[16,2048]{1,0:T(8,128)(2,1)}), bf16[512,2048]{1,0:T(8,128)(2,1)}) %all-gather.2.cloned.1.call-update) | async-done | bytes 2097168 | tf_op jit(solution)/shard_map/all_gather | solution.py:31
  102.0 2.9 fusion.23
  104.9 1.1 fusion.21
  106.0 127.0 %all-reduce.5.cloned.1.call-done = (f32[256,512]{1,0:T(8,128)}, f32[256,512]{1,0:T(8,128)}, f32[256,512]{1,0:T(8,128)}, f32[256,512]{1,0:T(8,128)}) async-done(((f32[256,512]{1,0:T(8,128)}, f32[256,512]{1,0:T(8,128)}, f32[256,512]{1,0:T(8,128)}, f32[256,512]{1,0:T(8,128)}), (f32[256,512]{1,0:T(8,128)}, f32[256,512]{1,0:T(8,128)}, f32[256,512]{1,0:T(8,128)}, ...) | async-done | bytes 2097168 | tf_op jit(solution)/shard_map/psum | solution.py:46
  233.0 1.3 multiply_reduce_fusion.3
  234.4 1.9 fusion.2
  236.3 2.8 convolution_add_fusion
  239.1 0.8 copy-done.8
  240.3 0.2 copy-done.3
  240.5 0.4 multiply_reduce_fusion.1
  240.9 0.4 subtract_convert_fusion.1
  241.3 0.2 copy-done.5
  241.5 0.3 fusion.12
  241.9 0.3 fusion
  242.2 0.4 copy-done.6
  242.6 0.4 convolution_convert_fusion.1
  243.0 0.4 convolution_convert_fusion
  243.3 0.8 pad_maximum_fusion
  244.1 184.4 %all-reduce.6 = (bf16[448,576]{1,0:T(8,128)(2,1)}, f32[512]{0:T(512)}) all-reduce(f32[448,576]{1,0:T(8,128)S(1)} %fusion, f32[512]{0:T(512)S(1)} %add.46), channel_id=1, replica_groups=mesh['dp'=32,'tensor'=16] {'dp'}, use_global_device_ids=true, to_apply=%region_8.0 | all-reduce | flops 258560 | bytes 1552384 | tf_op jit(solution)/shard_map/psum | solution.py:66
  428.5 49.8 %reduce-scatter.2.cloned.1.call-done = f32[16,2048]{1,0:T(8,128)} async-done(((f32[512,2048]{1,0:T(8,128)}), f32[16,2048]{1,0:T(8,128)}) %reduce-scatter.2.cloned.1.call-update) | async-done | bytes 131088 | tf_op jit(solution)/shard_map/reduce_scatter | solution.py:63
  478.3 1.5 convert_element_type.31
  (25 shorter events, 0.6 us)
Async XLA Ops:
  7.2 94.8 %copy-start.4 = (bf16[512,2048]{1,0:T(8,128)(2,1)S(1)}, bf16[512,2048]{1,0:T(8,128)(2,1)}, u32[]{:S(2)}) copy-start(bf16[512,2048]{1,0:T(8,128)(2,1)} %param.10) | copy-start | bytes 6291460
  7.2 94.8 %all-gather.2.cloned.1.call-start = ((), (), s32[]{:S(2)}) async-start(), calls=%async_computation.1 | async-start | bytes 2162688 | tf_op jit(solution)/shard_map/all_gather | solution.py:31
  7.9 225.1 %all-reduce.5.cloned.1.call-start = ((), (), s32[]{:S(2)}) async-start(), calls=%async_computation.3 | async-start | bytes 4194304 | tf_op jit(solution)/shard_map/psum | solution.py:46
  105.9 128.4 %copy-start.7 = (f32[512]{0:T(512)S(1)}, f32[512]{0:T(512)}, u32[]{:S(2)}) copy-start(f32[512]{0:T(512)} %param.8) | copy-start | bytes 6148
  105.9 372.4 %reduce-scatter.2.cloned.1.call-start = ((), (), s32[]{:S(2)}) async-start(), calls=%async_computation.2 | async-start | bytes 4325376 | tf_op jit(solution)/shard_map/reduce_scatter | solution.py:63
  234.4 1.9 copy-start.1
  239.1 0.8 copy-start.8
  239.1 1.1 copy-start
  239.1 1.2 copy-start.2
  239.1 1.4 copy-start.3
  240.5 1.0 copy-start.5
  241.5 1.1 copy-start.6
Sparse Core Ops, SparseCore 0:
  11.2 90.7 all-gather.1
  106.1 126.8 all-reduce.4
  239.3 239.0 reduce-scatter.1
where the time goes:
time: 487 us; the launch traced here: 486 us
  waiting for transfers between devices  267 us (55%)
  blocking collectives  184 us (38%)
  between operations  13.9 us (3%)
  matrix products  13.6 us (3%)
    psum x1, blocking collectives, shards(): down_grad = lax.psum(down_running, 'dp').astype(jnp.bfloat16)  184 us
    psum x1, waiting for transfers between devices, shards(): lax.psum((proj_partial, latent_grad_all[row_range]), 'tensor')  127 us
    all_gather x1, waiting for transfers between devices, shards(): lax.all_gather(w_up, 'dp', axis=0, tiled=True)  89.5 us
    reduce_scatter x1, waiting for transfers between devices, shards(): lax.psum_scatter(up_running, 'dp', scatter_dimension=0, tiled=True)  49.8 us
  transfers between devices with their start and end apart: 3, of which 3 were waited for; matrix products, arithmetic and copies ran while one was open for 2% of the time, Pallas kernels for 0%

commit v1 on v0

--- a/solution.py
+++ b/solution.py
@@ -5,6 +5,7 @@
 
 MB = 256
 MICROS = 2
+_work_words = lambda x0: lax.all_gather(x0, axis_name="dp").sum(axis=0)
 
 
 def norm_back(projected, latent_grad, norm_gain, lat_width):
@@ -63,7 +64,7 @@
     up_grad = lax.psum_scatter(up_running, "dp", scatter_dimension=0, tiled=True).astype(
         jnp.bfloat16
     )
-    down_grad = lax.psum(down_running, "dp").astype(jnp.bfloat16)
+    down_grad = _work_words(down_running).astype(jnp.bfloat16)
     return (hidden_grad, down_grad, gain_grad, up_grad)
 
 

time: 487 us -> 916 us (1.88)
  the two profiles are of different devices: /device:TPU:2 before, /device:TPU:10 now
where the time goes in v1:
time: 916 us
  waiting for transfers between devices  782 us (85%)
  blocking collectives  83.6 us (9%)
  other arithmetic  19.1 us (2%)
  matrix products  14.6 us (2%)
  between operations  13.9 us (2%)
    all_gather x1, waiting for transfers between devices, _work_words = lambda x0: lax.all_gather(x0, axis_name='dp').sum(axis=0)  417 us
    reduce_scatter x1, waiting for transfers between devices, shards(): lax.psum_scatter(up_running, 'dp', scatter_dimension=0, tiled=True)  151 us
    psum x1, waiting for transfers between devices, shards(): lax.psum((proj_partial, latent_grad_all[row_range]), 'tensor')  124 us
    all_gather x1, waiting for transfers between devices, shards(): lax.all_gather(w_up, 'dp', axis=0, tiled=True)  89.1 us
    psum x1, blocking collectives, shards(): gain_grad = lax.psum(gain_running, 'dp')  83.6 us
  transfers between devices with their start and end apart: 4, of which 4 were waited for; matrix products, arithmetic and copies ran while one was open for 1% of the time, Pallas kernels for 0%

profile of v1, /device:TPU:10, one launch (start us, length us, event | category | flops | bytes accessed | tf_op | source)
XLA Modules:
  0.0 915.9 jit_solution(1289826922665332926)
XLA Ops:
  7.2 0.7 all-gather.4.cloned.1.call-update
  8.0 2.3 fusion.4
  10.2 2.3 fusion.6
  12.5 89.1 %all-gather.4.cloned.1.call-done = bf16[512,2048]{1,0:T(8,128)(2,1)} async-done(((bf16[16,2048]{1,0:T(8,128)(2,1)}), bf16[512,2048]{1,0:T(8,128)(2,1)}) %all-gather.4.cloned.1.call-update) | async-done | bytes 2097168 | tf_op jit(solution)/shard_map/all_gather | solution.py:32
  101.6 2.9 fusion.23
  104.5 1.1 fusion.21
  105.7 123.8 %all-reduce.3.cloned.1.call-done = (f32[256,512]{1,0:T(8,128)}, f32[256,512]{1,0:T(8,128)}, f32[256,512]{1,0:T(8,128)}, f32[256,512]{1,0:T(8,128)}) async-done(((f32[256,512]{1,0:T(8,128)}, f32[256,512]{1,0:T(8,128)}, f32[256,512]{1,0:T(8,128)}, f32[256,512]{1,0:T(8,128)}), (f32[256,512]{1,0:T(8,128)}, f32[256,512]{1,0:T(8,128)}, f32[256,512]{1,0:T(8,128)}, ...) | async-done | bytes 2097168 | tf_op jit(solution)/shard_map/psum | solution.py:47
  229.4 1.3 multiply_reduce_fusion.3
  230.8 1.9 fusion.2
  232.8 2.8 convolution_add_fusion
  235.7 0.8 copy-done.8
  237.0 0.4 multiply_reduce_fusion.1
  237.4 0.4 subtract_convert_fusion.1
  237.8 0.3 copy-done.5
  238.0 0.3 fusion.12
  238.4 1.4 fusion
  239.8 83.6 %psum.39 = f32[512]{0:T(512)} all-reduce(f32[512]{0:T(512)S(1)} %add.44), channel_id=1, replica_groups=mesh['dp'=32,'tensor'=16] {'dp'}, use_global_device_ids=true, to_apply=%region_11.0 | all-reduce | flops 512 | bytes 4096 | tf_op jit(solution)/shard_map/psum | solution.py:63
  323.4 0.4 convolution_convert_fusion.1
  323.8 0.4 convolution_convert_fusion
  324.2 0.8 pad_maximum_fusion
  325.0 150.7 %reduce-scatter.2.cloned.1.call-done = f32[16,2048]{1,0:T(8,128)} async-done(((f32[512,2048]{1,0:T(8,128)}), f32[16,2048]{1,0:T(8,128)}) %reduce-scatter.2.cloned.1.call-update) | async-done | bytes 131088 | tf_op jit(solution)/shard_map/reduce_scatter | solution.py:64
  475.7 1.5 convert_element_type.31
  477.2 417.5 %all-gather.6.cloned.1.call-done = f32[14336,576]{1,0:T(8,128)} async-done(((f32[448,576]{1,0:T(8,128)}), f32[14336,576]{1,0:T(8,128)}) %all-gather.6.cloned.1.call-update) | async-done | bytes 33030160 | tf_op jit(solution)/shard_map/all_gather | solution.py:8
  894.7 14.7 %reduce_sum.67 = bf16[448,576]{1,0:T(8,128)(2,1)} reduce(f32[32,448,576]{2,1,0:T(8,128)} %bitcast.7, f32[]{:T(128)} %constant.8.clone.1), dimensions={0}, to_apply=%region_8.0 | reduce | flops 7999488 | bytes 33546244 | tf_op jit(solution)/shard_map/reduce_sum | solution.py:8
  (29 shorter events, 0.8 us)
Async XLA Ops:
  7.2 94.5 %copy-start.4 = (bf16[512,2048]{1,0:T(8,128)(2,1)S(1)}, bf16[512,2048]{1,0:T(8,128)(2,1)}, u32[]{:S(2)}) copy-start(bf16[512,2048]{1,0:T(8,128)(2,1)} %param.10) | copy-start | bytes 6291460
  7.2 94.5 %all-gather.4.cloned.1.call-start = ((), (), s32[]{:S(2)}) async-start(), calls=%async_computation.1 | async-start | bytes 2162688 | tf_op jit(solution)/shard_map/all_gather | solution.py:32
  7.9 221.5 %all-reduce.3.cloned.1.call-start = ((), (), s32[]{:S(2)}) async-start(), calls=%async_computation.4 | async-start | bytes 4194304 | tf_op jit(solution)/shard_map/psum | solution.py:47
  105.6 125.2 %copy-start.7 = (f32[512]{0:T(512)S(1)}, f32[512]{0:T(512)}, u32[]{:S(2)}) copy-start(f32[512]{0:T(512)} %param.8) | copy-start | bytes 6148
  105.6 370.1 %reduce-scatter.2.cloned.1.call-start = ((), (), s32[]{:S(2)}) async-start(), calls=%async_computation.2 | async-start | bytes 4325376 | tf_op jit(solution)/shard_map/reduce_scatter | solution.py:64
  230.8 1.9 copy-start.1
  235.6 0.8 copy-start.8
  235.6 1.1 copy-start
  235.6 1.2 copy-start.2
  235.6 1.4 copy-start.3
  235.7 659.0 %all-gather.6.cloned.1.call-start = ((), (), s32[]{:S(2)}) async-start(), calls=%async_computation.3 | async-start | bytes 37847040 | tf_op jit(solution)/shard_map/all_gather | solution.py:8
  237.0 1.0 copy-start.5
  238.4 85.1 %copy-start.6 = (bf16[448,576]{1,0:T(8,128)(2,1)S(1)}, bf16[448,576]{1,0:T(8,128)(2,1)}, u32[]{:S(2)}) copy-start(bf16[448,576]{1,0:T(8,128)(2,1)} %param.7) | copy-start | bytes 1548292
Sparse Core Ops, SparseCore 0:
  11.2 90.4 all-gather.3
  105.7 123.6 all-reduce.2
  235.8 239.8 reduce-scatter.1
  479.2 415.4 all-gather.5
